TPU v7x, 128 devices: a whole 4x4x4 slice. The times are simulated.
128 devices in a mesh: front: 8 (over z, core), panel: 16 (over x, y).
Axes of the slice: x: 4, y: 4, z: 4, core: 2. Of those that a mesh axis runs over, the one named last changes fastest.
Arguments:
- pivot_columns: float32 [8, 8192, 1024], P('front', 'panel')
- child_rows: bfloat16 [8, 16, 16, 4, 8192], P('front', 'panel'), may hold values from -0.375 to 0.375
- slot_rows: int32 [8, 16, 16, 4], P('front', 'panel'), may hold values from -1 to 511, as said below
- parents: int32 [8], replicated, may hold values from 0 to 7, as said below
- pivot_rhs: float32 [8, 1024, 128], P('front'), may hold values from -6 to 6
- boundary_solution: float32 [8, 8192, 128], P('front', 'panel'), may hold values from -6 to 6
Outputs:
- panel_factor: float32 [8, 8192, 1024], P('front', 'panel')
- update_matrix: bfloat16 [8, 8192, 7168], P('front', 'panel')
- front_solution: float32 [8, 8192, 128], P('front', 'panel')
- child_solution: float32 [8, 16, 16, 4, 128], P('front', 'panel')
Inputs may be any that keep to these rules, and one draw needn't show every extreme that they name: parents[c] is the front of this level into which child front c's rows are added; a front may take several children or none. `slot_rows`: the live slots of each tile of 4 slots come first; the rows that one child front sends to one destination device are distinct; for each child front one destination device receives full tiles from every source device.
All inputs are finite; a program needn't handle non-finite values.
Results may differ from a plain program's by a relative error of at most 0.007.
Values may be sent and summed in bfloat16 or wider, within the bound.
A program may use at most 192 MiB of HBM per device.

v0:
```python
import jax
import jax.numpy as jnp
from jax import lax
from jax.sharding import PartitionSpec as P

K = 512
NSTEP = 2


def spread(shard, axis, root):
    mine = lax.axis_index(axis) == root
    return lax.psum(jnp.where(mine, shard, jnp.zeros_like(shard)), axis)


def outer_rows(mine, piece):
    return lax.dot_general(
        mine, piece, (((1,), (1,)), ((), ())), preferred_element_type=jnp.float32
    )


def scatter_term(slots, rows, local_ids, width):
    onehot = (slots.reshape(-1)[None, :] == local_ids[:, None]).astype(jnp.bfloat16)
    return jnp.dot(onehot, rows.reshape(-1, width), preferred_element_type=jnp.float32)


def on_device(pivot_columns, child_rows, slot_rows, parents, pivot_rhs, boundary_solution):
    highest = lax.Precision.HIGHEST
    panel_index = lax.axis_index("panel")
    front_index = lax.axis_index("front")
    piv_cols = pivot_columns[0]
    row_count = piv_cols.shape[0]
    pivots = piv_cols.shape[1]
    width = child_rows.shape[-1]
    rhs_count = pivot_rhs.shape[-1]
    local_ids = jnp.arange(row_count, dtype=jnp.int32)
    glob_rows = panel_index * row_count + local_ids
    rows_out = child_rows[0, 0]
    slots_out = slot_rows[0, 0]
    routed_rows, routed_slots = (
        lax.all_to_all(rows_out, "panel", split_axis=0, concat_axis=0, tiled=True),
        lax.all_to_all(slots_out, "panel", split_axis=0, concat_axis=0, tiled=True),
    )
    piece_rows = lax.all_gather(routed_rows[None], "front", axis=0, tiled=True)
    piece_slots = lax.all_gather(routed_slots[None], "front", axis=0, tiled=True)
    keeping = parents == front_index

    def add_rows(current):
        kept_slots = jnp.where(keeping[:, None, None], piece_slots, -1)
        return scatter_term(kept_slots, piece_rows, local_ids, width)

    def keep_same(current):
        return current

    assembled = lax.cond(
        jnp.any(keeping), add_rows, keep_same, jnp.zeros((row_count, width), jnp.float32)
    )
    work = assembled + jnp.concatenate(
        [piv_cols, jnp.zeros((row_count, width - pivots), jnp.float32)], axis=1
    )
    identity_block = jnp.eye(K, dtype=jnp.float32)

    def factor_block(values):
        lower = jnp.linalg.cholesky(values)
        return lax.linalg.triangular_solve(lower, identity_block, left_side=True, lower=True)

    def empty_block(values):
        return jnp.zeros_like(values)

    factors = []
    inverses = []
    for panel_step in range(NSTEP):
        low_edge = panel_step * K
        high_edge = low_edge + K
        root_rank = low_edge // row_count
        offset = low_edge - root_rank * row_count
        pivot_block = work[offset : offset + K, low_edge:high_edge]
        inverse = lax.cond(panel_index == root_rank, factor_block, empty_block, pivot_block)
        inverse = spread(inverse, "panel", root_rank)
        column = jnp.dot(work[:, low_edge:high_edge], inverse.T, precision=highest)
        column = jnp.where(glob_rows[:, None] >= low_edge, column, 0.0)
        packed = column.astype(jnp.bfloat16)
        factors.append(column)
        inverses.append(inverse)
        work = work - outer_rows(packed, lax.all_gather(packed, "panel", axis=0, tiled=True))
    factor_all = jnp.concatenate(factors, axis=1)
    trailing = work[:, pivots:]
    update_matrix = jnp.where(glob_rows[:, None] >= pivots, trailing, 0.0).astype(jnp.bfloat16)
    known = boundary_solution[0]
    right_side = pivot_rhs[0]

    def local_values(solved):
        extended = jnp.concatenate([solved, jnp.zeros((row_count, rhs_count), jnp.float32)], axis=0)
        begin = jnp.minimum(panel_index * row_count, pivots)
        segment = lax.dynamic_slice_in_dim(extended, begin, row_count)
        return jnp.where(glob_rows[:, None] < pivots, segment, known)

    solved = jnp.zeros((pivots, rhs_count), jnp.float32)
    contract_rows = (((0,), (0,)), ((), ()))
    for panel_step in reversed(range(NSTEP)):
        low_edge = panel_step * K
        high_edge = low_edge + K
        current = local_values(solved)
        masked = jnp.where(glob_rows[:, None] >= high_edge, factors[panel_step], 0.0)
        partial_sum = lax.dot_general(masked, current, contract_rows, precision=highest)
        carried = lax.psum(partial_sum, "panel")
        value = lax.dot_general(
            inverses[panel_step],
            right_side[low_edge:high_edge] - carried,
            contract_rows,
            precision=highest,
        )
        solved = solved.at[low_edge:high_edge].set(value)
    front_values = local_values(solved)
    slot_onehot = (routed_slots[..., None] == local_ids).astype(jnp.float32)
    piece = lax.all_gather(front_values[None], "front", axis=0, tiled=True)
    piece_count = piece.shape[0]
    weights = (jnp.arange(piece_count, dtype=jnp.int32) == parents[front_index]).astype(jnp.float32)
    chosen = jnp.einsum("n,nrh->rh", weights, piece, precision=highest)
    slot_values = jnp.einsum("psr,rh->psh", slot_onehot, chosen, precision=highest)
    child_values = lax.all_to_all(slot_values, "panel", split_axis=0, concat_axis=0, tiled=True)
    return (factor_all[None], update_matrix[None], front_values[None], child_values[None, None])


def solution(mesh):
    in_specs = (
        P("front", "panel", None),
        P("front", "panel", None, None, None),
        P("front", "panel", None, None),
        P(),
        P("front", None, None),
        P("front", "panel", None),
    )
    out_specs = (
        P("front", "panel", None),
        P("front", "panel", None),
        P("front", "panel", None),
        P("front", "panel", None, None, None),
    )
    return jax.shard_map(
        on_device, mesh=mesh, in_specs=in_specs, out_specs=out_specs, check_vma=False
    )
```

profile of v0, /device:TPU:0, one launch (start us, length us, event | category | flops | bytes accessed | tf_op | source)
XLA Modules:
  0.0 1002.9 jit_solution(4517287727802942974)
XLA Ops:
  7.2 24.1 %all_to_all.19 = bf16[16,4,8192]{2,1,0:T(4,128)(2,1)} all-to-all(bf16[16,4,8192]{2,1,0:T(4,128)(2,1)} %bitcast.145), channel_id=1, replica_groups=mesh['front'=8,'panel'=16] {'panel'}, dimensions={0} | all-to-all | bytes 2097152 | tf_op jit(solution)/shard_map/all_to_all | solution.py:40
  38.6 5.4 all-to-all-done
  44.0 14.0 %all-gather = s32[128,1,4]{2,1,0:T(1,128)S(1)} all-gather(s32[16,1,4]{2,1,0:T(1,128)S(1)} %all-to-all-done), channel_id=2, replica_groups=mesh['front'=8,'panel'=16] {'front'}, dimensions={0}, use_global_device_ids=true | all-gather | bytes 2304 | tf_op jit(solution)/shard_map/all_gather | solution.py:44
  58.0 22.9 %all-gather.12.cloned.1.call-done = bf16[128,4,8192]{2,1,0:T(4,128)(2,1)} async-done(((bf16[16,4,8192]{2,1,0:T(4,128)(2,1)}), bf16[128,4,8192]{2,1,0:T(4,128)(2,1)}) %all-gather.12.cloned.1.call-update) | async-done | bytes 8388624 | tf_op jit(solution)/shard_map/all_gather | solution.py:43
  80.9 24.2 %conditional.3 = (f32[512,8192]{1,0:T(8,128)}) conditional(s32[]{:T(128)} %convert_element_type.26, () %tuple.36, (pred[8]{0:T(512)(128)(4,1)S(1)}, s32[8,16,4]{2,1,0:T(8,128)S(1)}, s32[512]{0:T(512)S(1)}, bf16[8,16,4,8192]{3,2,1,0:T(4,128)(2,1)}) %tuple.137), branch_computations={%region_1.0_spmd, %region_2.3_spmd} | conditional | flops 4295229952 | bytes 41955344 | solution.py:54
  81.0 12.5 %reshape.120 = bf16[512,8192]{1,0:T(8,128)(2,1)} reshape(bf16[8,16,4,8192]{3,2,1,0:T(4,128)(2,1)} %get-tuple-element.54) | data formatting | bytes 16777216 | tf_op jit(solution)/shard_map/cond/branch_1_fun/reshape | solution.py:23
  93.6 11.5 %fusion = f32[512,8192]{1,0:T(8,128)} fusion(bf16[512,8192]{1,0:T(8,128)(2,1)} %reshape.120, s32[512]{0:T(512)S(1)} %eq.3, s32[512]{0:T(512)S(1)} %get-tuple-element.53), kind=kOutput, calls=%fused_computation | convolution fusion | flops 4295229440 | bytes 25169920 | tf_op jit(solution)/shard_map/cond/branch_1_fun/dot_general | solution.py:23
  105.0 7.0 pad_add_fusion
  112.0 5.7 copy-done
  117.8 141.4 %conditional.4 = (f32[512,512]{0,1:T(8,128)}) conditional(s32[]{:T(128)} %convert_element_type.27, () %tuple.38, (f32[512,512]{1,0:T(8,128)S(1)}, f32[512,512]{1,0:T(8,128)S(1)}) %tuple.39), branch_computations={%region_3.4_spmd, %region_4.15_spmd} | conditional | flops 1412760064 | bytes 26743068 | solution.py:77
  119.7 11.7 %cholesky.286 = f32[128,128]{1,0:T(8,128)S(1)} custom-call(f32[128,128]{1,0:T(8,128)S(1)} %cholesky.426), custom_call_target="Cholesky" | custom-call | tf_op jit(solution)/shard_map/cond/branch_1_fun/jit(cholesky)/cholesky | solution.py:63
  131.4 9.8 custom-call.27
  143.9 11.7 %cholesky.305 = f32[128,128]{1,0:T(8,128)S(1)} custom-call(f32[128,128]{1,0:T(8,128)S(1)} %cholesky.430), custom_call_target="Cholesky" | custom-call | tf_op jit(solution)/shard_map/cond/branch_1_fun/jit(cholesky)/cholesky | solution.py:63
  157.7 10.0 %custom-call.28 = f32[1,128,128]{1,2,0:T(8,128)S(1)} custom-call(f32[1,128,128]{2,1,0:T(8,128)S(1)} %get-tuple-element.139), custom_call_target="InvertDiagBlocksLowerTriangular" | custom-call | tf_op jit(solution)/shard_map/cond/branch_1_fun/jit(cholesky)/cholesky | solution.py:63
  169.3 11.7 %cholesky.326 = f32[128,128]{1,0:T(8,128)S(1)} custom-call(f32[128,128]{1,0:T(8,128)S(1)} %cholesky.435), custom_call_target="Cholesky" | custom-call | tf_op jit(solution)/shard_map/cond/branch_1_fun/jit(cholesky)/cholesky | solution.py:63
  182.3 9.8 custom-call.29
  193.6 11.7 %cholesky.343 = f32[128,128]{1,0:T(8,128)S(1)} custom-call(f32[128,128]{1,0:T(8,128)S(1)} %convolution_subtract_fusion.5), custom_call_target="Cholesky" | custom-call | tf_op jit(solution)/shard_map/cond/branch_1_fun/jit(cholesky)/cholesky | solution.py:63
  207.2 8.0 while.6
  215.3 39.3 %custom-call.30 = f32[4,128,128]{1,2,0:T(8,128)S(1)} custom-call(f32[4,128,128]{2,1,0:T(8,128)S(1)} %get-tuple-element.77), custom_call_target="InvertDiagBlocksLowerTriangular" | custom-call | tf_op jit(solution)/shard_map/cond/branch_1_fun/triangular_solve/custom-call.3 | solution.py:64
  261.7 82.1 %all-reduce.11.cloned.1.call-done = f32[512,512]{0,1:T(8,128)} async-done(((f32[512,512]{0,1:T(8,128)}), f32[512,512]{0,1:T(8,128)}) %all-reduce.11.cloned.1.call-update) | async-done | bytes 1048592 | tf_op jit(solution)/shard_map/psum | solution.py:12
  348.1 77.5 %all-gather.8.cloned.1.call-done = bf16[8192,512]{0,1:T(8,128)(2,1)} async-done(((bf16[512,512]{0,1:T(8,128)(2,1)}), bf16[8192,512]{0,1:T(8,128)(2,1)}) %all-gather.8.cloned.1.call-update) | async-done | bytes 8388624 | tf_op jit(solution)/shard_map/all_gather | solution.py:84
  425.6 18.7 %convolution_subtract_fusion.12 = f32[512,8192]{1,0:T(8,128)} fusion(f32[512,8192]{1,0:T(8,128)} %copy-done, bf16[512,512]{0,1:T(8,128)(2,1)} %get-tuple-element.163, bf16[8192,512]{0,1:T(8,128)(2,1)} %all-gather.8.cloned.1.call-done), kind=kOutput, calls=%fused_computation.141 | convolution fusion | flops 4299161600 | bytes 42467328 | tf_op jit(solution)/shard_map/dot_general | solution.py:16
  445.6 8.3 conditional.5
  455.1 237.6 %all-reduce.13.cloned.1.call-done = f32[512,512]{0,1:T(8,128)} async-done(((f32[512,512]{0,1:T(8,128)}), f32[512,512]{0,1:T(8,128)}) %all-reduce.13.cloned.1.call-update) | async-done | bytes 1048592 | tf_op jit(solution)/shard_map/psum | solution.py:12
  698.8 83.3 %all-reduce.15.cloned.1.call-done = f32[512,128]{1,0:T(8,128)} async-done(((f32[512,128]{1,0:T(8,128)}), f32[512,128]{1,0:T(8,128)}) %all-reduce.15.cloned.1.call-update) | async-done | bytes 262160 | tf_op jit(solution)/shard_map/psum | solution.py:105
  786.3 83.5 %all-reduce.17.cloned.1.call-done = f32[512,128]{1,0:T(8,128)} async-done(((f32[512,128]{1,0:T(8,128)}), f32[512,128]{1,0:T(8,128)}) %all-reduce.17.cloned.1.call-update) | async-done | bytes 262160 | tf_op jit(solution)/shard_map/psum | solution.py:105
  874.5 23.5 %all-gather.14.cloned.1.call-done = f32[4096,128]{1,0:T(8,128)} async-done(((f32[512,128]{1,0:T(8,128)}), f32[4096,128]{1,0:T(8,128)}) %all-gather.14.cloned.1.call-update) | async-done | bytes 2097168 | tf_op jit(solution)/shard_map/all_gather | solution.py:115
  898.0 4.4 fusion.67
  903.3 7.1 all-to-all-start.2
  918.0 60.9 %all-gather.10.cloned.1.call-done = bf16[8192,512]{0,1:T(8,128)(2,1)} async-done(((bf16[512,512]{0,1:T(8,128)(2,1)}), bf16[8192,512]{0,1:T(8,128)(2,1)}) %all-gather.10.cloned.1.call-update) | async-done | bytes 8388624 | tf_op jit(solution)/shard_map/all_gather | solution.py:84
  978.8 7.1 fusion.112
  986.0 9.0 fusion.66
  (104 shorter events, 63.4 us)
Async XLA Ops:
  7.2 73.7 %all-gather.12.cloned.1.call-start = ((), (), s32[]{:S(2)}) async-start(), calls=%async_computation.9 | async-start | bytes 9437184 | tf_op jit(solution)/shard_map/all_gather | solution.py:43
  32.7 11.3 %all-to-all-start = ((s32[16,1,4]{2,1,0:T(1,128)}), s32[16,1,4]{2,1,0:T(1,128)S(1)}, u32[]{:S(2)}, u32[]{:S(2)}) async-start(s32[16,1,4]{2,1,0:T(1,128)} %copy.30), calls=%async_computation | async-start | bytes 16384 | tf_op jit(solution)/shard_map/all_to_all | solution.py:41
  36.5 307.3 %all-reduce.11.cloned.1.call-start = ((), (), s32[]{:S(2)}) async-start(), calls=%async_computation.3 | async-start | bytes 2097152 | tf_op jit(solution)/shard_map/psum | solution.py:12
  112.0 5.7 copy-start
  118.7 1.0 copy-start.2
  261.6 164.0 %all-gather.8.cloned.1.call-start = ((), (), s32[]{:S(2)}) async-start(), calls=%async_computation.4 | async-start | bytes 8912896 | tf_op jit(solution)/shard_map/all_gather | solution.py:84
  348.0 344.7 %all-reduce.13.cloned.1.call-start = ((), (), s32[]{:S(2)}) async-start(), calls=%async_computation.5 | async-start | bytes 2097152 | tf_op jit(solution)/shard_map/psum | solution.py:12
  445.6 251.4 %copy-start.4 = (f32[1,512,128]{2,1,0:T(8,128)S(1)}, f32[1,512,128]{2,1,0:T(8,128)}, u32[]{:S(2)}) copy-start(f32[1,512,128]{2,1,0:T(8,128)} %param.24) | copy-start | bytes 786436
  453.8 328.3 %copy-start.6 = (f32[1,1024,128]{2,1,0:T(8,128)S(1)}, f32[1,1024,128]{2,1,0:T(8,128)}, u32[]{:S(2)}) copy-start(f32[1,1024,128]{2,1,0:T(8,128)} %param.23) | copy-start | bytes 1572868
  453.8 419.9 %copy-start.7 = (s32[8]{0:T(128)S(1)}, s32[8]{0:T(128)}, u32[]{:S(2)}) copy-start(s32[8]{0:T(128)} %param.22) | copy-start | bytes 100
  454.9 327.2 %all-reduce.15.cloned.1.call-start = ((), (), s32[]{:S(2)}) async-start(), calls=%async_computation.7 | async-start | bytes 524288 | tf_op jit(solution)/shard_map/psum | solution.py:105
  698.8 171.0 %all-reduce.17.cloned.1.call-start = ((), (), s32[]{:S(2)}) async-start(), calls=%async_computation.8 | async-start | bytes 524288 | tf_op jit(solution)/shard_map/psum | solution.py:105
  784.4 194.4 %copy-start.1 = (bf16[512,512]{0,1:T(8,128)(2,1)S(1)}, bf16[512,512]{0,1:T(8,128)(2,1)}, u32[]{:S(2)}) copy-start(bf16[512,512]{0,1:T(8,128)(2,1)} %get-tuple-element.165) | copy-start | bytes 1572868
  786.2 111.8 %all-gather.14.cloned.1.call-start = ((), (), s32[]{:S(2)}) async-start(), calls=%async_computation.10 | async-start | bytes 2359296 | tf_op jit(solution)/shard_map/all_gather | solution.py:115
  873.0 105.8 %all-gather.10.cloned.1.call-start = ((), (), s32[]{:S(2)}) async-start(), calls=%async_computation.6 | async-start | bytes 8912896 | tf_op jit(solution)/shard_map/all_gather | solution.py:84
  903.3 14.6 %all-to-all-start.2 = ((f32[16,4,128]{2,1,0:T(4,128)}), f32[16,4,128]{2,1,0:T(4,128)S(1)}, u32[]{:S(2)}, u32[]{:S(2)}) async-start(f32[16,4,128]{2,1,0:T(4,128)} %copy.36), calls=%async_computation.2 | async-start | bytes 65536 | tf_op jit(solution)/shard_map/all_to_all | solution.py:120
Sparse Core Ops, SparseCore 0:
  31.4 49.3 all-gather.11
  261.7 82.0 all-reduce.10
  348.1 77.4 all-gather.7
  455.1 237.5 all-reduce.12
  698.9 83.2 all-reduce.14
  786.3 83.3 all-reduce.16
  873.2 24.8 all-gather.13
  900.1 78.6 all-gather.9
where the time goes:
time: 1010 us; the launch traced here: 1000 us
  waiting for transfers between devices  681 us (67%)
  other arithmetic  142 us (14%)
  matrix products  67.1 us (7%)
  blocking collectives  38.1 us (4%)
  local copies, waits for them, and re-layouts  37.7 us (4%)
  between operations  15.5 us (2%)
  starting transfers between devices  11.3 us (1%)
  loops' own time  10.5 us (1%)
    psum x2, waiting for transfers between devices, spread(): return lax.psum(jnp.where(mine, shard, jnp.zeros_like(shard)), axis)  320 us
    psum x2, waiting for transfers between devices, on_device(): carried = lax.psum(partial_sum, 'panel')  167 us
    all_gather x2, waiting for transfers between devices, on_device(): lax.all_gather(packed, 'panel', axis=0, tiled=True)  138 us
    another operation x14, other arithmetic, factor_block(): lower = jnp.linalg.cholesky(values)  78.6 us
    another operation x5, other arithmetic, factor_block(): lax.linalg.triangular_solve(lower, identity_block, left_side=True, lower=...  40 us
    dot_general x2, matrix products, outer_rows(): lax.dot_general(mine, piece, (((1,), (1,)), ((), ())), preferred_element_...  25.8 us
    all_to_all x1, blocking collectives, on_device(): lax.all_to_all(rows_out, 'panel', split_axis=0, concat_axis=0, tiled=True)  24.1 us
    all_gather x1, waiting for transfers between devices, on_device(): piece = lax.all_gather(front_values[None], 'front', axis=0, tiled=True)  23.5 us
  transfers between devices with their start and end apart: 10, of which 10 were waited for; matrix products, arithmetic and copies ran while one was open for 1% of the time, Pallas kernels for 0%

commit v1 on v0

--- a/solution.py
+++ b/solution.py
@@ -2,9 +2,17 @@
 import jax.numpy as jnp
 from jax import lax
 from jax.sharding import PartitionSpec as P
+from jax.lax import all_to_all, axis_size
 
 K = 512
 NSTEP = 2
+
+
+def list_matrix(array_here, link_axis):
+    g_now = tuple((array_here for _ in range(axis_size(link_axis))))
+    far_arr = jnp.stack(g_now)
+    piece_out = all_to_all(far_arr, link_axis, 0, 0)
+    return jnp.concatenate(piece_out, 0)
 
 
 def spread(shard, axis, root):
@@ -112,7 +120,7 @@
         solved = solved.at[low_edge:high_edge].set(value)
     front_values = local_values(solved)
     slot_onehot = (routed_slots[..., None] == local_ids).astype(jnp.float32)
-    piece = lax.all_gather(front_values[None], "front", axis=0, tiled=True)
+    piece = list_matrix(front_values[None], "front")
     piece_count = piece.shape[0]
     weights = (jnp.arange(piece_count, dtype=jnp.int32) == parents[front_index]).astype(jnp.float32)
     chosen = jnp.einsum("n,nrh->rh", weights, piece, precision=highest)

time: 1010 us -> 981 us (0.971)
  waiting for transfers between devices: 681 us -> 647 us
    all_gather x2, waiting for transfers between devices: 138 us -> 103 us  [on_device(): lax.all_gather(packed, 'panel', axis=0, tiled=True)]
    all_to_all x0 -> x1, waiting for transfers between devices: none -> 26.6 us  [list_matrix(): piece_out = all_to_all(far_arr, link_axis, 0, 0)]
    all_gather x1 -> x0, waiting for transfers between devices: 23.5 us -> none  [on_device(): piece = lax.all_gather(front_values[None], 'front', axis=0, tiled=True)]
  transfers between devices with their start and end apart: 10 -> 10, of which waited for: 10 -> 10; matrix products, arithmetic and copies ran while one was open for 1% -> 2% of each run, Pallas kernels for 0% -> 0%
where the time goes in v1:
time: 981 us; the launch traced here: 975 us
  waiting for transfers between devices  647 us (66%)
  other arithmetic  142 us (14%)
  matrix products  67.9 us (7%)
  local copies, waits for them, and re-layouts  39.2 us (4%)
  blocking collectives  38.1 us (4%)
  between operations  15.5 us (2%)
  starting transfers between devices  13.7 us (1%)
  loops' own time  10.6 us (1%)
    psum x2, waiting for transfers between devices, spread(): return lax.psum(jnp.where(mine, shard, jnp.zeros_like(shard)), axis)  320 us
    psum x2, waiting for transfers between devices, on_device(): carried = lax.psum(partial_sum, 'panel')  166 us
    all_gather x2, waiting for transfers between devices, on_device(): lax.all_gather(packed, 'panel', axis=0, tiled=True)  103 us
    another operation x14, other arithmetic, factor_block(): lower = jnp.linalg.cholesky(values)  78.6 us
    another operation x5, other arithmetic, factor_block(): lax.linalg.triangular_solve(lower, identity_block, left_side=True, lower=...  40 us
    all_to_all x1, waiting for transfers between devices, list_matrix(): piece_out = all_to_all(far_arr, link_axis, 0, 0)  26.6 us
    dot_general x2, matrix products, outer_rows(): lax.dot_general(mine, piece, (((1,), (1,)), ((), ())), preferred_element_...  25.8 us
    all_to_all x1, blocking collectives, on_device(): lax.all_to_all(rows_out, 'panel', split_axis=0, concat_axis=0, tiled=True)  24.1 us
  transfers between devices with their start and end apart: 10, of which 10 were waited for; matrix products, arithmetic and copies ran while one was open for 2% of the time, Pallas kernels for 0%

profile of v1, /device:TPU:0, one launch (start us, length us, event | category | flops | bytes accessed | tf_op | source)
XLA Modules:
  0.0 974.8 jit_solution(18408929871049664572)
XLA Ops:
  7.2 24.1 %all_to_all.24 = bf16[16,4,8192]{2,1,0:T(4,128)(2,1)} all-to-all(bf16[16,4,8192]{2,1,0:T(4,128)(2,1)} %bitcast.144), channel_id=1, replica_groups=mesh['front'=8,'panel'=16] {'panel'}, dimensions={0} | all-to-all | bytes 2097152 | tf_op jit(solution)/shard_map/all_to_all | solution.py:48
  38.6 5.4 all-to-all-done
  44.0 14.0 %all-gather = s32[128,1,4]{2,1,0:T(1,128)S(1)} all-gather(s32[16,1,4]{2,1,0:T(1,128)S(1)} %all-to-all-done), channel_id=2, replica_groups=mesh['front'=8,'panel'=16] {'front'}, dimensions={0}, use_global_device_ids=true | all-gather | bytes 2304 | tf_op jit(solution)/shard_map/all_gather | solution.py:52
  58.0 22.9 %all-gather.10.cloned.1.call-done = bf16[128,4,8192]{2,1,0:T(4,128)(2,1)} async-done(((bf16[16,4,8192]{2,1,0:T(4,128)(2,1)}), bf16[128,4,8192]{2,1,0:T(4,128)(2,1)}) %all-gather.10.cloned.1.call-update) | async-done | bytes 8388624 | tf_op jit(solution)/shard_map/all_gather | solution.py:51
  80.9 24.2 %conditional.3 = (f32[512,8192]{1,0:T(8,128)}) conditional(s32[]{:T(128)} %convert_element_type.26, () %tuple.36, (pred[8]{0:T(512)(128)(4,1)S(1)}, s32[8,16,4]{2,1,0:T(8,128)S(1)}, s32[512]{0:T(512)S(1)}, bf16[8,16,4,8192]{3,2,1,0:T(4,128)(2,1)}) %tuple.135), branch_computations={%region_1.0_spmd, %region_2.3_spmd} | conditional | flops 4295229952 | bytes 41955344 | solution.py:62
  81.0 12.5 %reshape.124 = bf16[512,8192]{1,0:T(8,128)(2,1)} reshape(bf16[8,16,4,8192]{3,2,1,0:T(4,128)(2,1)} %get-tuple-element.54) | data formatting | bytes 16777216 | tf_op jit(solution)/shard_map/cond/branch_1_fun/reshape | solution.py:31
  93.6 11.5 %fusion = f32[512,8192]{1,0:T(8,128)} fusion(bf16[512,8192]{1,0:T(8,128)(2,1)} %reshape.124, s32[512]{0:T(512)S(1)} %eq.3, s32[512]{0:T(512)S(1)} %get-tuple-element.53), kind=kOutput, calls=%fused_computation | convolution fusion | flops 4295229440 | bytes 25169920 | tf_op jit(solution)/shard_map/cond/branch_1_fun/dot_general | solution.py:31
  105.0 7.0 pad_add_fusion
  112.0 5.7 copy-done
  117.8 141.4 %conditional.4 = (f32[512,512]{0,1:T(8,128)}) conditional(s32[]{:T(128)} %convert_element_type.27, () %tuple.38, (f32[512,512]{1,0:T(8,128)S(1)}, f32[512,512]{1,0:T(8,128)S(1)}) %tuple.39), branch_computations={%region_3.4_spmd, %region_4.15_spmd} | conditional | flops 1412760064 | bytes 26743068 | solution.py:85
  119.7 11.7 %cholesky.286 = f32[128,128]{1,0:T(8,128)S(1)} custom-call(f32[128,128]{1,0:T(8,128)S(1)} %cholesky.426), custom_call_target="Cholesky" | custom-call | tf_op jit(solution)/shard_map/cond/branch_1_fun/jit(cholesky)/cholesky | solution.py:71
  131.4 9.8 %custom-call.27 = f32[1,128,128]{1,2,0:T(8,128)S(1)} custom-call(f32[1,128,128]{2,1,0:T(8,128)S(1)} %get-tuple-element.142), custom_call_target="InvertDiagBlocksLowerTriangular" | custom-call | tf_op jit(solution)/shard_map/cond/branch_1_fun/jit(cholesky)/cholesky | solution.py:71
  143.9 11.7 %cholesky.305 = f32[128,128]{1,0:T(8,128)S(1)} custom-call(f32[128,128]{1,0:T(8,128)S(1)} %cholesky.430), custom_call_target="Cholesky" | custom-call | tf_op jit(solution)/shard_map/cond/branch_1_fun/jit(cholesky)/cholesky | solution.py:71
  157.7 10.0 %custom-call.28 = f32[1,128,128]{1,2,0:T(8,128)S(1)} custom-call(f32[1,128,128]{2,1,0:T(8,128)S(1)} %get-tuple-element.139), custom_call_target="InvertDiagBlocksLowerTriangular" | custom-call | tf_op jit(solution)/shard_map/cond/branch_1_fun/jit(cholesky)/cholesky | solution.py:71
  169.3 11.7 %cholesky.326 = f32[128,128]{1,0:T(8,128)S(1)} custom-call(f32[128,128]{1,0:T(8,128)S(1)} %cholesky.435), custom_call_target="Cholesky" | custom-call | tf_op jit(solution)/shard_map/cond/branch_1_fun/jit(cholesky)/cholesky | solution.py:71
  182.3 9.8 %custom-call.29 = f32[1,128,128]{1,2,0:T(8,128)S(1)} custom-call(f32[1,128,128]{2,1,0:T(8,128)S(1)} %get-tuple-element.136), custom_call_target="InvertDiagBlocksLowerTriangular" | custom-call | tf_op jit(solution)/shard_map/cond/branch_1_fun/jit(cholesky)/cholesky | solution.py:71
  193.6 11.7 %cholesky.343 = f32[128,128]{1,0:T(8,128)S(1)} custom-call(f32[128,128]{1,0:T(8,128)S(1)} %convolution_subtract_fusion.5), custom_call_target="Cholesky" | custom-call | tf_op jit(solution)/shard_map/cond/branch_1_fun/jit(cholesky)/cholesky | solution.py:71
  207.2 8.0 while.6
  215.3 39.3 %custom-call.30 = f32[4,128,128]{1,2,0:T(8,128)S(1)} custom-call(f32[4,128,128]{2,1,0:T(8,128)S(1)} %get-tuple-element.77), custom_call_target="InvertDiagBlocksLowerTriangular" | custom-call | tf_op jit(solution)/shard_map/cond/branch_1_fun/triangular_solve/custom-call.3 | solution.py:72
  261.7 82.1 %all-reduce.11.cloned.1.call-done = f32[512,512]{0,1:T(8,128)} async-done(((f32[512,512]{0,1:T(8,128)}), f32[512,512]{0,1:T(8,128)}) %all-reduce.11.cloned.1.call-update) | async-done | bytes 1048592 | tf_op jit(solution)/shard_map/psum | solution.py:20
  348.1 77.5 %all-gather.6.cloned.1.call-done = bf16[8192,512]{0,1:T(8,128)(2,1)} async-done(((bf16[512,512]{0,1:T(8,128)(2,1)}), bf16[8192,512]{0,1:T(8,128)(2,1)}) %all-gather.6.cloned.1.call-update) | async-done | bytes 8388624 | tf_op jit(solution)/shard_map/all_gather | solution.py:92
  425.6 18.7 %convolution_subtract_fusion.12 = f32[512,8192]{1,0:T(8,128)} fusion(f32[512,8192]{1,0:T(8,128)} %copy-done, bf16[512,512]{0,1:T(8,128)(2,1)} %get-tuple-element.163, bf16[8192,512]{0,1:T(8,128)(2,1)} %all-gather.6.cloned.1.call-done), kind=kOutput, calls=%fused_computation.141 | convolution fusion | flops 4299161600 | bytes 42467328 | tf_op jit(solution)/shard_map/dot_general | solution.py:24
  445.6 8.4 conditional.5
  455.3 237.5 %all-reduce.13.cloned.1.call-done = f32[512,512]{0,1:T(8,128)} async-done(((f32[512,512]{0,1:T(8,128)}), f32[512,512]{0,1:T(8,128)}) %all-reduce.13.cloned.1.call-update) | async-done | bytes 1048592 | tf_op jit(solution)/shard_map/psum | solution.py:20
  698.9 83.3 %all-reduce.15.cloned.1.call-done = f32[512,128]{1,0:T(8,128)} async-done(((f32[512,128]{1,0:T(8,128)}), f32[512,128]{1,0:T(8,128)}) %all-reduce.15.cloned.1.call-update) | async-done | bytes 262160 | tf_op jit(solution)/shard_map/psum | solution.py:113
  788.0 82.8 %all-reduce.17.cloned.1.call-done = f32[512,128]{1,0:T(8,128)} async-done(((f32[512,128]{1,0:T(8,128)}), f32[512,128]{1,0:T(8,128)}) %all-reduce.17.cloned.1.call-update) | async-done | bytes 262160 | tf_op jit(solution)/shard_map/psum | solution.py:113
  880.6 26.6 %all-to-all-done.2 = f32[8,1,512,128]{3,2,1,0:T(8,128)} async-done(((f32[8,1,512,128]{3,2,1,0:T(8,128)}), f32[8,1,512,128]{3,2,1,0:T(8,128)}, u32[]{:S(2)}, u32[]{:S(2)}) %all-to-all-start.2) | async-done | bytes 2097184 | tf_op jit(solution)/shard_map/all_to_all | solution.py:14
  907.2 4.5 fusion.67
  912.6 5.2 all-to-all-start.3
  925.3 25.4 %all-gather.8.cloned.1.call-done = bf16[8192,512]{0,1:T(8,128)(2,1)} async-done(((bf16[512,512]{0,1:T(8,128)(2,1)}), bf16[8192,512]{0,1:T(8,128)(2,1)}) %all-gather.8.cloned.1.call-update) | async-done | bytes 8388624 | tf_op jit(solution)/shard_map/all_gather | solution.py:92
  950.7 7.1 fusion.112
  957.9 9.0 fusion.66
  (106 shorter events, 70.2 us)
Async XLA Ops:
  7.2 73.7 %all-gather.10.cloned.1.call-start = ((), (), s32[]{:S(2)}) async-start(), calls=%async_computation.10 | async-start | bytes 9437184 | tf_op jit(solution)/shard_map/all_gather | solution.py:51
  32.7 11.3 %all-to-all-start = ((s32[16,1,4]{2,1,0:T(1,128)}), s32[16,1,4]{2,1,0:T(1,128)S(1)}, u32[]{:S(2)}, u32[]{:S(2)}) async-start(s32[16,1,4]{2,1,0:T(1,128)} %copy.30), calls=%async_computation | async-start | bytes 16384 | tf_op jit(solution)/shard_map/all_to_all | solution.py:49
  36.5 307.3 %all-reduce.11.cloned.1.call-start = ((), (), s32[]{:S(2)}) async-start(), calls=%async_computation.4 | async-start | bytes 2097152 | tf_op jit(solution)/shard_map/psum | solution.py:20
  112.0 5.7 copy-start
  118.7 1.0 copy-start.3
  261.6 164.0 %all-gather.6.cloned.1.call-start = ((), (), s32[]{:S(2)}) async-start(), calls=%async_computation.5 | async-start | bytes 8912896 | tf_op jit(solution)/shard_map/all_gather | solution.py:92
  348.0 344.7 %all-reduce.13.cloned.1.call-start = ((), (), s32[]{:S(2)}) async-start(), calls=%async_computation.6 | async-start | bytes 2097152 | tf_op jit(solution)/shard_map/psum | solution.py:20
  445.6 251.4 %copy-start.5 = (f32[1,512,128]{2,1,0:T(8,128)S(1)}, f32[1,512,128]{2,1,0:T(8,128)}, u32[]{:S(2)}) copy-start(f32[1,512,128]{2,1,0:T(8,128)} %param.24) | copy-start | bytes 786436
  454.0 416.8 %copy-start.2 = (f32[512,512]{0,1:T(8,128)S(1)}, f32[512,512]{0,1:T(8,128)}, u32[]{:S(2)}) copy-start(f32[512,512]{0,1:T(8,128)} %all-reduce.11.cloned.1.call-done) | copy-start | bytes 3145732
  455.1 327.1 %all-reduce.15.cloned.1.call-start = ((), (), s32[]{:S(2)}) async-start(), calls=%async_computation.8 | async-start | bytes 524288 | tf_op jit(solution)/shard_map/psum | solution.py:113
  697.0 182.9 %copy-start.8 = (s32[8]{0:T(128)S(1)}, s32[8]{0:T(128)}, u32[]{:S(2)}) copy-start(s32[8]{0:T(128)} %param.22) | copy-start | bytes 100
  698.8 172.0 %all-reduce.17.cloned.1.call-start = ((), (), s32[]{:S(2)}) async-start(), calls=%async_computation.9 | async-start | bytes 524288 | tf_op jit(solution)/shard_map/psum | solution.py:113
  787.3 163.5 %all-gather.8.cloned.1.call-start = ((), (), s32[]{:S(2)}) async-start(), calls=%async_computation.7 | async-start | bytes 8912896 | tf_op jit(solution)/shard_map/all_gather | solution.py:92
  874.0 48.2 %copy-start.6 = (f32[512,128]{1,0:T(8,128)}, f32[512,128]{1,0:T(8,128)S(1)}, u32[]{:S(2)}) copy-start(f32[512,128]{1,0:T(8,128)S(1)} %fusion.82) | copy-start | bytes 786436
  874.0 76.8 %copy-start.1 = (bf16[512,512]{0,1:T(8,128)(2,1)S(1)}, bf16[512,512]{0,1:T(8,128)(2,1)}, u32[]{:S(2)}) copy-start(bf16[512,512]{0,1:T(8,128)(2,1)} %get-tuple-element.165) | copy-start | bytes 1572868
  875.4 31.7 %all-to-all-start.2 = ((f32[8,1,512,128]{3,2,1,0:T(8,128)}), f32[8,1,512,128]{3,2,1,0:T(8,128)}, u32[]{:S(2)}, u32[]{:S(2)}) async-start(f32[8,1,512,128]{3,2,1,0:T(8,128)} %stack.3), calls=%async_computation.2 | async-start | bytes 4194304 | tf_op jit(solution)/shard_map/all_to_all | solution.py:14
  912.6 12.7 %all-to-all-start.3 = ((f32[16,4,128]{2,1,0:T(4,128)}), f32[16,4,128]{2,1,0:T(4,128)S(1)}, u32[]{:S(2)}, u32[]{:S(2)}) async-start(f32[16,4,128]{2,1,0:T(4,128)} %copy.36), calls=%async_computation.3 | async-start | bytes 65536 | tf_op jit(solution)/shard_map/all_to_all | solution.py:128
Sparse Core Ops, SparseCore 0:
  31.4 49.3 all-gather.9
  261.7 82.0 all-reduce.10
  348.1 77.4 all-gather.5
  455.2 237.5 all-reduce.12
  698.9 83.2 all-reduce.14
  787.4 83.3 all-reduce.16
  872.9 77.8 all-gather.7
